TPU v7x, 32 devices: a whole 2x2x4 slice. The times are simulated.
32 devices in a mesh: mem: 4 (over y, core), sub: 8 (over z, x).
Axes of the slice: x: 2, y: 2, z: 4, core: 2. Of those that a mesh axis runs over, the one named last changes fastest.
Arguments:
- prior_sample_array: float32 [80, 8, 24, 512], P('mem', 'sub'), may hold values from -6 to 6
- courant_x: float32 [8, 512], P('sub'), may hold values from -0.3 to 0.3
- courant_y: float32 [8, 512], P('sub'), may hold values from -0.3 to 0.3
- diffusion: float32 [8, 512], P('sub'), may hold values from 0.02 to 0.09
- obs_cell: int32 [4, 128], replicated, may hold values from 0 to 4095
- obs_value: float32 [4, 128], replicated, may hold values from -6 to 6
- obs_error: float32 [4, 128], replicated, may hold values from 0.2 to 1
- obs_weight: float32 [4, 128, 24], replicated, may hold values from -1.25 to 1.25
- taper_radius: float32 [4, 128], replicated, may hold values from 64 to 256
Outputs:
- analysis: float32 [80, 8, 24, 512], P(None, 'sub', None, 'mem')
All inputs are finite; a program needn't handle non-finite values.
Results may differ from a plain program's by a relative error of at most 0.0003.
Values sent between devices are 32-bit elements; how exact they have to be, the bound alone decides.
No kernel may reach another device: no remote copies, remote signals or barrier semaphores. Data moves between devices by JAX's collectives and lax.ppermute only.
A program may use at most 64 MiB of HBM per device.

v0:
```python
import jax
import jax.numpy as jnp
from jax import lax
from jax.sharding import PartitionSpec as P

highest = lax.Precision.HIGHEST


def padded_2(shard, sides, width):
    for axis, dim in sides:
        size, length = (lax.axis_size(axis), shard.shape[dim])
        up = [(i, (i + 1) % size) for i in range(size - 1)]
        down = [(j, i) for i, j in up]
        last = lax.slice_in_dim(shard, length - width, length, axis=dim)
        first = lax.slice_in_dim(shard, 0, width, axis=dim)
        before = lax.ppermute(last, axis, up)
        after = lax.ppermute(first, axis, down)
        shard = jnp.concatenate([before, shard, after], axis=dim)
    return shard


def gaspari(delta_row, delta_col, cutoff_radius, width):
    cyclic_shifted = (delta_col + width // 2) % width - width // 2
    row_dist = delta_row.astype(jnp.float32)
    col_dist = cyclic_shifted.astype(jnp.float32)
    ratio = jnp.sqrt(row_dist * row_dist + col_dist * col_dist) / cutoff_radius
    inner = (((-0.25 * ratio + 0.5) * ratio + 0.625) * ratio - 5.0 / 3.0) * ratio * ratio + 1.0
    bounded = jnp.maximum(ratio, 1.0)
    outer = (
        ((((ratio / 12.0 - 0.5) * ratio + 0.625) * ratio + 5.0 / 3.0) * ratio - 5.0) * ratio
        + 4.0
        - 2.0 / (3.0 * bounded)
    )
    return jnp.where(ratio <= 1.0, inner, jnp.where(ratio < 2.0, outer, 0.0))


def carried_quantity(
    center,
    west_cells,
    east_cells,
    north_cells,
    southern_neighbours,
    flow_x,
    meridional_velocity,
    mixing,
):
    result = (
        center
        - jnp.maximum(flow_x, 0.0) * (center - west_cells)
        - jnp.minimum(flow_x, 0.0) * (east_cells - center)
    )
    result = (
        result
        - jnp.maximum(meridional_velocity, 0.0) * (center - southern_neighbours)
        - jnp.minimum(meridional_velocity, 0.0) * (north_cells - center)
    )
    return result + mixing * (
        east_cells + west_cells + north_cells + southern_neighbours - 4.0 * center
    )


def obs_factors(obs_prior, obs_value, obs_error):
    members = obs_prior.shape[1]
    average = jnp.mean(obs_prior, axis=1)
    anomaly = obs_prior - average[:, None]
    covariance = jnp.dot(anomaly, anomaly.T, precision=highest) / (members - 1) + jnp.diag(
        obs_error
    )
    factor = jnp.linalg.cholesky(covariance)
    innovation = (obs_value - average)[:, None]
    midpoint_values = lax.linalg.triangular_solve(factor, innovation, left_side=True, lower=True)
    solved = lax.linalg.triangular_solve(
        factor, midpoint_values, left_side=True, lower=True, transpose_a=True
    )
    shifted = factor + jnp.diag(jnp.sqrt(obs_error))
    reduced = lax.linalg.triangular_solve(shifted, anomaly, left_side=True, lower=True)
    squared = lax.linalg.triangular_solve(
        factor, reduced, left_side=True, lower=True, transpose_a=True
    )
    return (anomaly, solved - squared)


def local_prior(existing_grid_values, obs_rows, obs_cols, weights, row_start, col_start):
    rows_dev = existing_grid_values.shape[1]
    cols_dev = existing_grid_values.shape[3]
    local_rows = obs_rows - row_start
    local_cols = obs_cols - col_start
    owned = (
        (local_rows >= 0) & (local_rows < rows_dev) & (local_cols >= 0) & (local_cols < cols_dev)
    )
    picked = existing_grid_values[
        :, jnp.clip(local_rows, 0, rows_dev - 1), :, jnp.clip(local_cols, 0, cols_dev - 1)
    ]
    values = jnp.einsum("kmc,kc->km", picked, weights, precision=highest)
    return jnp.where(owned[:, None], values, 0.0)


def apply_update(existing_grid_values, obs_anomaly, coeffs, taper_cells, members):
    average = jnp.mean(existing_grid_values, axis=0)
    anomaly = existing_grid_values - average[None]
    cross_cov = jnp.einsum("mrcx,km->rcxk", anomaly, obs_anomaly, precision=highest) / (members - 1)
    gain = cross_cov * taper_cells[:, None, :, :]
    return existing_grid_values + jnp.einsum("rcxk,km->mrcx", gain, coeffs, precision=highest)


def shards(
    prior_sample_array,
    courant_x,
    courant_y,
    diffusion,
    obs_cell,
    obs_value,
    obs_error,
    obs_weight,
    taper_radius,
):
    width = courant_x.shape[1]
    rows_dev = prior_sample_array.shape[1]
    cols_dev = width // lax.axis_size("mem")
    members = prior_sample_array.shape[0] * lax.axis_size("mem")
    col_start = lax.axis_index("mem") * cols_dev
    row_start = lax.axis_index("sub") * rows_dev
    padded = padded_2(prior_sample_array, (("sub", 1),), 1)
    propagated_grids = carried_quantity(
        prior_sample_array,
        jnp.roll(prior_sample_array, 1, axis=3),
        jnp.roll(prior_sample_array, -1, axis=3),
        padded[:, 2:],
        padded[:, :-2],
        courant_x[:, None, :],
        courant_y[:, None, :],
        diffusion[:, None, :],
    )
    existing_grid_values = lax.all_to_all(
        propagated_grids, "mem", split_axis=3, concat_axis=0, tiled=True
    )
    row_ids = row_start + jnp.arange(rows_dev, dtype=jnp.int32)
    col_ids = col_start + jnp.arange(cols_dev, dtype=jnp.int32)
    obs_rows = obs_cell // width
    obs_cols = obs_cell % width
    batches = obs_cell.shape[0]

    def taper_cells(batch_index):
        return gaspari(
            row_ids[:, None, None] - obs_rows[batch_index][None, None, :],
            col_ids[None, :, None] - obs_cols[batch_index][None, None, :],
            taper_radius[batch_index][None, None, :],
            width,
        )

    for batch_index in range(batches):
        obs_prior = lax.psum(
            local_prior(
                existing_grid_values,
                obs_rows[batch_index],
                obs_cols[batch_index],
                obs_weight[batch_index],
                row_start,
                col_start,
            ),
            ("mem", "sub"),
        )
        obs_anomaly, coeffs = obs_factors(obs_prior, obs_value[batch_index], obs_error[batch_index])
        existing_grid_values = apply_update(
            existing_grid_values, obs_anomaly, coeffs, taper_cells(batch_index), members
        )
    return existing_grid_values


def solution(mesh):
    return jax.shard_map(
        shards,
        mesh=mesh,
        in_specs=(
            P("mem", "sub", None, None),
            P("sub", None),
            P("sub", None),
            P("sub", None),
            P(),
            P(),
            P(),
            P(),
            P(),
        ),
        out_specs=P(None, "sub", None, "mem"),
        check_vma=False,
    )
```

profile of v0, /device:TPU:0, one launch (start us, length us, event | category | flops | bytes accessed | tf_op | source)
XLA Modules:
  0.0 428.5 jit_solution(3687478982285887635)
XLA Ops:
  0.0 5.9 %collective-permute-start = (f32[20,1,24,512]{3,2,1,0:T(8,128)}, f32[20,1,24,512]{3,2,1,0:T(8,128)}, u32[]{:S(2)}, u32[]{:S(2)}) collective-permute-start(f32[20,1,24,512]{3,2,1,0:T(8,128)} %param.18), channel_id=1, source_target_pairs={{0,1},{1,2},{2,3},{3,4},{4,5},{5,6},{6,7},{8,9},{9,10},{10,11},{11... | collective-permute-start | bytes 2949128 | tf_op jit(solution)/shard_map/ppermute | solution.py:16
  14.5 32.9 %collective-permute-done = f32[20,1,24,512]{3,2,1,0:T(8,128)} collective-permute-done((f32[20,1,24,512]{3,2,1,0:T(8,128)}, f32[20,1,24,512]{3,2,1,0:T(8,128)}, u32[]{:S(2)}, u32[]{:S(2)}) %collective-permute-start) | collective-permute-done | bytes 983072 | tf_op jit(solution)/shard_map/ppermute | solution.py:16
  48.3 2.4 multiply_add_fusion
  50.7 4.3 copy.87
  54.9 6.5 %reshape.1524 = f32[4,1,61440]{2,1,0:T(1,128)} reshape(f32[512,1,20,24]{3,2,1,0:T(8,128)} %bitcast.330) | data formatting | bytes 1966080
  61.5 4.1 all-to-all-start
  68.4 10.9 %all-to-all-done = f32[4,1,61440]{2,1,0:T(1,128)S(1)} async-done(((f32[4,1,61440]{2,1,0:T(1,128)}), f32[4,1,61440]{2,1,0:T(1,128)S(1)}, u32[]{:S(2)}, u32[]{:S(2)}) %all-to-all-start) | async-done | bytes 983072 | tf_op jit(solution)/shard_map/all_to_all | solution.py:134
  79.8 3.5 reduce.20
  83.3 6.0 %reshape.1525 = f32[512,1,20,24]{3,2,1,0:T(8,128)} reshape(f32[4,61440]{1,0:T(4,128)S(1)} %reduce.20) | data formatting | bytes 1966080
  89.4 5.6 %copy.88 = f32[20,1,24,512]{3,1,2,0:T(1,128)S(1)} copy(f32[20,1,24,512]{2,0,1,3:T(8,128)} %bitcast.331) | data formatting | bytes 1966080 | tf_op jit(solution)/shard_map/all_to_all | solution.py:134
  99.2 41.8 %psum.28 = f32[128,80]{0,1:T(8,128)S(1)} all-reduce(f32[128,80]{0,1:T(8,128)S(1)} %broadcast_select_fusion.3), channel_id=1, replica_groups=mesh['mem'=4,'sub'=8] {'mem','sub'}, use_global_device_ids=true, to_apply=%region_0.1 | all-reduce | flops 10240 | bytes 81920 | tf_op jit(solution)/shard_map/psum | solution.py:152
  143.0 11.7 %cholesky.74 = f32[128,128]{1,0:T(8,128)S(1)} custom-call(f32[128,128]{1,0:T(8,128)S(1)} %copy.93), custom_call_target="Cholesky" | custom-call | tf_op jit(solution)/shard_map/jit(cholesky)/cholesky | solution.py:69
  156.1 9.8 %custom-call.36 = f32[1,128,128]{1,2,0:T(8,128)S(1)} custom-call(f32[1,128,128]{2,1,0:T(8,128)S(1)} %get-tuple-element.21), custom_call_target="InvertDiagBlocksLowerTriangular" | custom-call | tf_op jit(solution)/shard_map/triangular_solve/custom-call.3 | solution.py:76
  166.1 9.8 %custom-call.35 = f32[1,128,128]{1,2,0:T(8,128)S(1)} custom-call(f32[1,128,128]{2,1,0:T(8,128)S(1)} %get-tuple-element.20), custom_call_target="InvertDiagBlocksLowerTriangular" | custom-call | tf_op jit(solution)/shard_map/triangular_solve/custom-call.2 | solution.py:72
  176.4 2.6 fusion.31
  179.3 2.8 fusion.186
  184.5 40.4 %psum.29 = f32[128,80]{0,1:T(8,128)S(1)} all-reduce(f32[128,80]{0,1:T(8,128)S(1)} %broadcast_select_fusion.2), channel_id=1, replica_groups=mesh['mem'=4,'sub'=8] {'mem','sub'}, use_global_device_ids=true, to_apply=%region_5.11 | all-reduce | flops 10240 | bytes 81920 | tf_op jit(solution)/shard_map/psum | solution.py:152
  225.5 11.7 %cholesky.85 = f32[128,128]{1,0:T(8,128)S(1)} custom-call(f32[128,128]{1,0:T(8,128)S(1)} %copy.98), custom_call_target="Cholesky" | custom-call | tf_op jit(solution)/shard_map/jit(cholesky)/cholesky | solution.py:69
  238.7 9.8 %custom-call.40 = f32[1,128,128]{1,2,0:T(8,128)S(1)} custom-call(f32[1,128,128]{2,1,0:T(8,128)S(1)} %get-tuple-element.19), custom_call_target="InvertDiagBlocksLowerTriangular" | custom-call | tf_op jit(solution)/shard_map/triangular_solve/custom-call.3 | solution.py:76
  248.7 9.8 %custom-call.39 = f32[1,128,128]{1,2,0:T(8,128)S(1)} custom-call(f32[1,128,128]{2,1,0:T(8,128)S(1)} %get-tuple-element.18), custom_call_target="InvertDiagBlocksLowerTriangular" | custom-call | tf_op jit(solution)/shard_map/triangular_solve/custom-call.2 | solution.py:72
  258.9 2.6 fusion.37
  266.2 40.3 %psum.30 = f32[128,80]{0,1:T(8,128)S(1)} all-reduce(f32[128,80]{0,1:T(8,128)S(1)} %broadcast_select_fusion.1), channel_id=1, replica_groups=mesh['mem'=4,'sub'=8] {'mem','sub'}, use_global_device_ids=true, to_apply=%region_8.14 | all-reduce | flops 10240 | bytes 81920 | tf_op jit(solution)/shard_map/psum | solution.py:152
  307.1 11.7 %cholesky.96 = f32[128,128]{1,0:T(8,128)S(1)} custom-call(f32[128,128]{1,0:T(8,128)S(1)} %copy.101), custom_call_target="Cholesky" | custom-call | tf_op jit(solution)/shard_map/jit(cholesky)/cholesky | solution.py:69
  320.2 9.8 %custom-call.44 = f32[1,128,128]{1,2,0:T(8,128)S(1)} custom-call(f32[1,128,128]{2,1,0:T(8,128)S(1)} %get-tuple-element.17), custom_call_target="InvertDiagBlocksLowerTriangular" | custom-call | tf_op jit(solution)/shard_map/triangular_solve/custom-call.3 | solution.py:76
  330.2 9.8 %custom-call.43 = f32[1,128,128]{1,2,0:T(8,128)S(1)} custom-call(f32[1,128,128]{2,1,0:T(8,128)S(1)} %get-tuple-element.16), custom_call_target="InvertDiagBlocksLowerTriangular" | custom-call | tf_op jit(solution)/shard_map/triangular_solve/custom-call.2 | solution.py:72
  340.4 2.6 fusion.35
  343.3 1.9 fusion.188
  347.7 40.6 %psum.31 = f32[128,80]{0,1:T(8,128)S(1)} all-reduce(f32[128,80]{0,1:T(8,128)S(1)} %broadcast_select_fusion), channel_id=1, replica_groups=mesh['mem'=4,'sub'=8] {'mem','sub'}, use_global_device_ids=true, to_apply=%region_11.17 | all-reduce | flops 10240 | bytes 81920 | tf_op jit(solution)/shard_map/psum | solution.py:152
  388.9 11.7 %cholesky.107 = f32[128,128]{1,0:T(8,128)S(1)} custom-call(f32[128,128]{1,0:T(8,128)S(1)} %copy.104), custom_call_target="Cholesky" | custom-call | tf_op jit(solution)/shard_map/jit(cholesky)/cholesky | solution.py:69
  402.2 9.8 %custom-call.48 = f32[1,128,128]{1,2,0:T(8,128)S(1)} custom-call(f32[1,128,128]{2,1,0:T(8,128)S(1)} %get-tuple-element.15), custom_call_target="InvertDiagBlocksLowerTriangular" | custom-call | tf_op jit(solution)/shard_map/triangular_solve/custom-call.3 | solution.py:76
  412.2 9.8 %custom-call.47 = f32[1,128,128]{1,2,0:T(8,128)S(1)} custom-call(f32[1,128,128]{2,1,0:T(8,128)S(1)} %get-tuple-element.14), custom_call_target="InvertDiagBlocksLowerTriangular" | custom-call | tf_op jit(solution)/shard_map/triangular_solve/custom-call.2 | solution.py:72
  422.4 2.6 fusion.33
  (161 shorter events, 41.5 us)
Async XLA Ops:
  0.0 14.1 %copy-start.8 = (f32[20,1,24,512]{3,2,1,0:T(8,128)S(1)}, f32[20,1,24,512]{3,2,1,0:T(8,128)}, u32[]{:S(2)}) copy-start(f32[20,1,24,512]{3,2,1,0:T(8,128)} %param.18) | copy-start | bytes 2949124
  0.0 47.4 %collective-permute-start = (f32[20,1,24,512]{3,2,1,0:T(8,128)}, f32[20,1,24,512]{3,2,1,0:T(8,128)}, u32[]{:S(2)}, u32[]{:S(2)}) collective-permute-start(f32[20,1,24,512]{3,2,1,0:T(8,128)} %param.18), channel_id=1, source_target_pairs={{0,1},{1,2},{2,3},{3,4},{4,5},{5,6},{6,7},{8,9},{9,10},{10,11},{11... | collective-permute-start | bytes 2949128 | tf_op jit(solution)/shard_map/ppermute | solution.py:16
  5.9 41.4 %collective-permute-start.1 = (f32[20,1,24,512]{3,2,1,0:T(8,128)}, f32[20,1,24,512]{3,2,1,0:T(8,128)S(1)}, u32[]{:S(2)}, u32[]{:S(2)}) collective-permute-start(f32[20,1,24,512]{3,2,1,0:T(8,128)} %param.18), channel_id=1, source_target_pairs={{1,0},{2,1},{3,2},{4,3},{5,4},{6,5},{7,6},{9,8},{10,9},{11,10},{12... | collective-permute-start | bytes 2949128 | tf_op jit(solution)/shard_map/ppermute | solution.py:17
  14.1 34.2 %copy-start.15 = (f32[1,512]{1,0:T(1,128)S(1)}, f32[1,512]{1,0:T(1,128)}, u32[]{:S(2)}) copy-start(f32[1,512]{1,0:T(1,128)} %param.21) | copy-start | bytes 6148
  47.4 0.9 copy-start.10
  61.5 6.4 %copy-start.28 = (f32[4,128]{1,0:T(4,128)S(1)}, f32[4,128]{1,0:T(4,128)}, u32[]{:S(2)}) copy-start(f32[4,128]{1,0:T(4,128)} %param.26) | copy-start | bytes 6148
  61.5 17.8 %all-to-all-start = ((f32[4,1,61440]{2,1,0:T(1,128)}), f32[4,1,61440]{2,1,0:T(1,128)S(1)}, u32[]{:S(2)}, u32[]{:S(2)}) async-start(f32[4,1,61440]{2,1,0:T(1,128)} %reshape.1524), calls=%async_computation | async-start | bytes 1966080 | tf_op jit(solution)/shard_map/all_to_all | solution.py:134
  94.9 0.9 copy-start.9
  95.9 1.0 copy-start.6
  97.7 1.5 copy-start.19
  97.7 44.8 %copy-start.27 = (f32[128]{0:T(128)S(1)}, f32[128]{0:T(128)}, u32[]{:S(2)}) copy-start(f32[128]{0:T(128)} %get-tuple-element.52) | copy-start | bytes 1540
  97.7 57.7 %copy-start.26 = (f32[128]{0:T(128)S(1)}, f32[128]{0:T(128)}, u32[]{:S(2)}) copy-start(f32[128]{0:T(128)} %get-tuple-element.49) | copy-start | bytes 1540
  99.1 76.8 %copy-start.13 = (f32[4,128]{1,0:T(4,128)S(1)}, f32[4,128]{1,0:T(4,128)}, u32[]{:S(2)}) copy-start(f32[4,128]{1,0:T(4,128)} %param.23) | copy-start | bytes 6148
  99.1 77.2 %copy-start.7 = (f32[4,20,1,24,128]{4,3,1,0,2:T(8,128)S(1)}, f32[4,20,1,24,128]{4,3,1,0,2:T(8,128)}, u32[]{:S(2)}) copy-start(f32[4,20,1,24,128]{4,3,1,0,2:T(8,128)} %copy-done.6) | copy-start | bytes 2949124
  182.1 0.9 copy-start.2
  183.0 0.8 copy-start.11
  183.9 0.7 copy-start.18
  183.9 41.1 %copy-start.25 = (f32[128]{0:T(128)S(1)}, f32[128]{0:T(128)}, u32[]{:S(2)}) copy-start(f32[128]{0:T(128)} %get-tuple-element.51) | copy-start | bytes 1540
  183.9 54.1 %copy-start.24 = (f32[128]{0:T(128)S(1)}, f32[128]{0:T(128)}, u32[]{:S(2)}) copy-start(f32[128]{0:T(128)} %get-tuple-element.48) | copy-start | bytes 1540
  183.9 75.0 %copy-start.12 = (f32[24,128]{1,0:T(8,128)S(1)}, f32[24,128]{1,0:T(8,128)}, u32[]{:S(2)}) copy-start(f32[24,128]{1,0:T(8,128)} %get-tuple-element.64) | copy-start | bytes 36868
  183.9 75.0 %copy-start.3 = (f32[80,24,128]{2,0,1:T(8,128)S(1)}, f32[80,24,128]{2,0,1:T(8,128)}, u32[]{:S(2)}) copy-start(f32[80,24,128]{2,0,1:T(8,128)} %copy-done.2) | copy-start | bytes 2949124
  263.7 0.9 copy-start.4
  265.5 0.7 copy-start.17
  265.5 41.0 %copy-start.23 = (f32[128]{0:T(128)S(1)}, f32[128]{0:T(128)}, u32[]{:S(2)}) copy-start(f32[128]{0:T(128)} %get-tuple-element.53) | copy-start | bytes 1540
  265.5 54.0 %copy-start.22 = (f32[128]{0:T(128)S(1)}, f32[128]{0:T(128)}, u32[]{:S(2)}) copy-start(f32[128]{0:T(128)} %get-tuple-element.47) | copy-start | bytes 1540
  265.5 74.9 %copy-start.5 = (f32[80,24,128]{2,0,1:T(8,128)S(1)}, f32[80,24,128]{2,0,1:T(8,128)}, u32[]{:S(2)}) copy-start(f32[80,24,128]{2,0,1:T(8,128)} %copy-done.4) | copy-start | bytes 2949124
  345.3 0.9 copy-start
  347.1 0.7 copy-start.16
  347.1 41.3 %copy-start.21 = (f32[128]{0:T(128)S(1)}, f32[128]{0:T(128)}, u32[]{:S(2)}) copy-start(f32[128]{0:T(128)} %get-tuple-element.50) | copy-start | bytes 1540
  347.1 54.3 %copy-start.20 = (f32[128]{0:T(128)S(1)}, f32[128]{0:T(128)}, u32[]{:S(2)}) copy-start(f32[128]{0:T(128)} %get-tuple-element.46) | copy-start | bytes 1540
  347.1 74.9 %copy-start.14 = (f32[4,128]{1,0:T(4,128)S(1)}, f32[4,128]{1,0:T(4,128)}, u32[]{:S(2)}) copy-start(f32[4,128]{1,0:T(4,128)} %param.23) | copy-start | bytes 6148
  347.1 75.3 %copy-start.1 = (f32[80,24,128]{2,0,1:T(8,128)S(1)}, f32[80,24,128]{2,0,1:T(8,128)}, u32[]{:S(2)}) copy-start(f32[80,24,128]{2,0,1:T(8,128)} %copy-done) | copy-start | bytes 2949124
where the time goes:
time: 432 us; the launch traced here: 428 us
  blocking collectives  163 us (38%)
  other arithmetic  145 us (34%)
  waiting for transfers between devices  43.8 us (10%)
  local copies, waits for them, and re-layouts  41.1 us (10%)
  matrix products  23.1 us (5%)
  starting transfers between devices  11.3 us (3%)
    psum x4, blocking collectives, shards(): lax.psum(local_prior(existing_grid_values, obs_rows[batch_index], obs_col...  163 us
    another operation x12, other arithmetic, obs_factors(): factor = jnp.linalg.cholesky(covariance)  49.7 us
    another operation x8, other arithmetic, obs_factors(): lax.linalg.triangular_solve(factor, midpoint_values, left_side=True, lowe...  42.2 us
    another operation x4, other arithmetic, obs_factors(): lax.linalg.triangular_solve(shifted, anomaly, left_side=True, lower=True)  39.2 us
    ppermute x1, waiting for transfers between devices, padded_2(): before = lax.ppermute(last, axis, up)  32.9 us
    unnamed x64, local copies, waits for them, and re-layouts  17.7 us
    all_to_all x1, waiting for transfers between devices, shards(): lax.all_to_all(propagated_grids, 'mem', split_axis=3, concat_axis=0, tile...  10.9 us
    dot_general x4, matrix products, apply_update(): jnp.einsum('mrcx,km->rcxk', anomaly, obs_anomaly, precision=highest)  10.5 us
  transfers between devices with their start and end apart: 3, of which 2 were waited for; matrix products, arithmetic and copies ran while one was open for 2% of the time, Pallas kernels for 0%

commit v1 on v0

--- a/solution.py
+++ b/solution.py
@@ -4,6 +4,18 @@
 from jax.sharding import PartitionSpec as P
 
 highest = lax.Precision.HIGHEST
+
+
+def in_blocks(x, dim, size):
+    shape = x.shape
+    blocks = x.reshape(*shape[:dim], size, shape[dim] // size, *shape[dim + 1 :])
+    return jnp.moveaxis(blocks, dim, 0)
+
+
+def joined_along(parts, dim):
+    lengths = list(parts.shape[1:])
+    lengths[dim] *= parts.shape[0]
+    return jnp.moveaxis(parts, 0, dim).reshape(lengths)
 
 
 def padded_2(shard, sides, width):
@@ -131,9 +143,14 @@
         courant_y[:, None, :],
         diffusion[:, None, :],
     )
-    existing_grid_values = lax.all_to_all(
-        propagated_grids, "mem", split_axis=3, concat_axis=0, tiled=True
-    )
+    count, position = (lax.axis_size("mem"), lax.axis_index("mem"))
+    parts = in_blocks(propagated_grids, 3, count)
+    done = [parts[position]]
+    for step in range(1, count):
+        sent = parts[position ^ step]
+        done.append(lax.ppermute(sent, "mem", [(i_2, i_2 ^ step) for i_2 in range(count)]))
+    parts = jnp.stack(done)[position ^ jnp.arange(count)]
+    existing_grid_values = joined_along(parts, 0)
     row_ids = row_start + jnp.arange(rows_dev, dtype=jnp.int32)
     col_ids = col_start + jnp.arange(cols_dev, dtype=jnp.int32)
     obs_rows = obs_cell // width

time: 432 us -> 404 us (0.935)
  local copies, waits for them, and re-layouts: 41.1 us -> 18.2 us
    unnamed x64 -> x56, local copies, waits for them, and re-layouts: 17.7 us -> 3.26 us
    all_to_all x1 -> x0, waiting for transfers between devices: 10.9 us -> none  [shards(): lax.all_to_all(propagated_grids, 'mem', split_axis=3, concat_axis=0, tile...]
    ppermute x0 -> x3, waiting for transfers between devices: none -> 9.48 us  [shards(): lax.ppermute(sent, 'mem', [(i_2, i_2 ^ step) for i_2 in range(count)])]
    all_to_all x4 -> x0, local copies, waits for them, and re-layouts: 6.76 us -> none  [shards(): lax.all_to_all(propagated_grids, 'mem', split_axis=3, concat_axis=0, tile...]
  transfers between devices with their start and end apart: 3 -> 5, of which waited for: 2 -> 3; matrix products, arithmetic and copies ran while one was open for 2% -> 3% of each run, Pallas kernels for 0% -> 0%
where the time goes in v1:
time: 404 us; the launch traced here: 398 us
  blocking collectives  164 us (41%)
  other arithmetic  141 us (35%)
  waiting for transfers between devices  40.9 us (10%)
  matrix products  23.2 us (6%)
  local copies, waits for them, and re-layouts  18.2 us (5%)
  starting transfers between devices  9.13 us (2%)
    psum x4, blocking collectives, shards(): lax.psum(local_prior(existing_grid_values, obs_rows[batch_index], obs_col...  164 us
    another operation x12, other arithmetic, obs_factors(): factor = jnp.linalg.cholesky(covariance)  49.7 us
    another operation x8, other arithmetic, obs_factors(): lax.linalg.triangular_solve(factor, midpoint_values, left_side=True, lowe...  42.1 us
    another operation x4, other arithmetic, obs_factors(): lax.linalg.triangular_solve(shifted, anomaly, left_side=True, lower=True)  39.2 us
    ppermute x1, waiting for transfers between devices, padded_2(): before = lax.ppermute(last, axis, up)  31.4 us
    dot_general x4, matrix products, apply_update(): jnp.einsum('mrcx,km->rcxk', anomaly, obs_anomaly, precision=highest)  10.5 us
    ppermute x3, waiting for transfers between devices, shards(): lax.ppermute(sent, 'mem', [(i_2, i_2 ^ step) for i_2 in range(count)])  9.48 us
    dot_general x4, matrix products, apply_update(): jnp.einsum('rcxk,km->mrcx', gain, coeffs, precision=highest)  8.39 us
  transfers between devices with their start and end apart: 5, of which 3 were waited for; matrix products, arithmetic and copies ran while one was open for 3% of the time, Pallas kernels for 0%

profile of v1, /device:TPU:0, one launch (start us, length us, event | category | flops | bytes accessed | tf_op | source)
XLA Modules:
  0.0 397.8 jit_solution(13758184502898599711)
XLA Ops:
  0.0 5.9 %collective-permute-start = (f32[20,1,24,512]{3,2,1,0:T(8,128)}, f32[20,1,24,512]{3,2,1,0:T(8,128)}, u32[]{:S(2)}, u32[]{:S(2)}) collective-permute-start(f32[20,1,24,512]{3,2,1,0:T(8,128)} %param.18), channel_id=1, source_target_pairs={{0,1},{1,2},{2,3},{3,4},{4,5},{5,6},{6,7},{8,9},{9,10},{10,11},{11... | collective-permute-start | bytes 2949128 | tf_op jit(solution)/shard_map/ppermute | solution.py:28
  9.9 1.4 fusion.184
  15.9 31.4 %collective-permute-done = f32[20,1,24,512]{3,2,1,0:T(8,128)} collective-permute-done((f32[20,1,24,512]{3,2,1,0:T(8,128)}, f32[20,1,24,512]{3,2,1,0:T(8,128)}, u32[]{:S(2)}, u32[]{:S(2)}) %collective-permute-start) | collective-permute-done | bytes 983072 | tf_op jit(solution)/shard_map/ppermute | solution.py:28
  47.4 2.4 multiply_add_fusion
  51.2 1.5 collective-permute-start.3
  55.2 4.1 %collective-permute-done.4 = f32[20,1,24,128]{3,2,0,1:T(8,128)S(1)} collective-permute-done((f32[20,1,24,128]{3,2,0,1:T(8,128)S(1)}, f32[20,1,24,128]{3,2,0,1:T(8,128)S(1)}, u32[]{:S(2)}, u32[]{:S(2)}) %collective-permute-start.4) | collective-permute-done | bytes 245792 | tf_op jit(solution)/shard_map/ppermute | solution.py:151
  59.3 5.3 %collective-permute-done.3 = f32[20,1,24,128]{3,2,0,1:T(8,128)S(1)} collective-permute-done((f32[20,1,24,128]{3,2,0,1:T(8,128)S(1)}, f32[20,1,24,128]{3,2,0,1:T(8,128)S(1)}, u32[]{:S(2)}, u32[]{:S(2)}) %collective-permute-start.3) | collective-permute-done | bytes 245792 | tf_op jit(solution)/shard_map/ppermute | solution.py:151
  67.2 1.4 multiply_reduce_fusion.3
  68.7 42.0 %psum.28 = f32[128,80]{0,1:T(8,128)S(1)} all-reduce(f32[128,80]{0,1:T(8,128)S(1)} %broadcast_select_fusion.3), channel_id=1, replica_groups=mesh['mem'=4,'sub'=8] {'mem','sub'}, use_global_device_ids=true, to_apply=%region_0.1 | all-reduce | flops 10240 | bytes 81920 | tf_op jit(solution)/shard_map/psum | solution.py:169
  111.4 11.7 %cholesky.74 = f32[128,128]{1,0:T(8,128)S(1)} custom-call(f32[128,128]{1,0:T(8,128)S(1)} %copy.43), custom_call_target="Cholesky" | custom-call | tf_op jit(solution)/shard_map/jit(cholesky)/cholesky | solution.py:81
  124.6 9.8 %custom-call.36 = f32[1,128,128]{1,2,0:T(8,128)S(1)} custom-call(f32[1,128,128]{2,1,0:T(8,128)S(1)} %get-tuple-element.25), custom_call_target="InvertDiagBlocksLowerTriangular" | custom-call | tf_op jit(solution)/shard_map/triangular_solve/custom-call.3 | solution.py:88
  134.6 9.8 %custom-call.35 = f32[1,128,128]{1,2,0:T(8,128)S(1)} custom-call(f32[1,128,128]{2,1,0:T(8,128)S(1)} %get-tuple-element.24), custom_call_target="InvertDiagBlocksLowerTriangular" | custom-call | tf_op jit(solution)/shard_map/triangular_solve/custom-call.2 | solution.py:84
  144.9 2.6 fusion.31
  147.8 2.8 fusion.187
  153.1 41.4 %psum.29 = f32[128,80]{0,1:T(8,128)S(1)} all-reduce(f32[128,80]{0,1:T(8,128)S(1)} %broadcast_select_fusion.2), channel_id=1, replica_groups=mesh['mem'=4,'sub'=8] {'mem','sub'}, use_global_device_ids=true, to_apply=%region_5.11 | all-reduce | flops 10240 | bytes 81920 | tf_op jit(solution)/shard_map/psum | solution.py:169
  195.0 11.7 %cholesky.85 = f32[128,128]{1,0:T(8,128)S(1)} custom-call(f32[128,128]{1,0:T(8,128)S(1)} %copy.48), custom_call_target="Cholesky" | custom-call | tf_op jit(solution)/shard_map/jit(cholesky)/cholesky | solution.py:81
  208.0 9.8 %custom-call.40 = f32[1,128,128]{1,2,0:T(8,128)S(1)} custom-call(f32[1,128,128]{2,1,0:T(8,128)S(1)} %get-tuple-element.23), custom_call_target="InvertDiagBlocksLowerTriangular" | custom-call | tf_op jit(solution)/shard_map/triangular_solve/custom-call.3 | solution.py:88
  218.0 9.8 %custom-call.39 = f32[1,128,128]{1,2,0:T(8,128)S(1)} custom-call(f32[1,128,128]{2,1,0:T(8,128)S(1)} %get-tuple-element.22), custom_call_target="InvertDiagBlocksLowerTriangular" | custom-call | tf_op jit(solution)/shard_map/triangular_solve/custom-call.2 | solution.py:84
  228.2 2.6 fusion.37
  231.1 1.9 fusion.188
  235.5 39.5 %psum.30 = f32[128,80]{0,1:T(8,128)S(1)} all-reduce(f32[128,80]{0,1:T(8,128)S(1)} %broadcast_select_fusion.1), channel_id=1, replica_groups=mesh['mem'=4,'sub'=8] {'mem','sub'}, use_global_device_ids=true, to_apply=%region_8.14 | all-reduce | flops 10240 | bytes 81920 | tf_op jit(solution)/shard_map/psum | solution.py:169
  275.5 11.7 %cholesky.96 = f32[128,128]{1,0:T(8,128)S(1)} custom-call(f32[128,128]{1,0:T(8,128)S(1)} %copy.51), custom_call_target="Cholesky" | custom-call | tf_op jit(solution)/shard_map/jit(cholesky)/cholesky | solution.py:81
  288.6 9.8 %custom-call.44 = f32[1,128,128]{1,2,0:T(8,128)S(1)} custom-call(f32[1,128,128]{2,1,0:T(8,128)S(1)} %get-tuple-element.21), custom_call_target="InvertDiagBlocksLowerTriangular" | custom-call | tf_op jit(solution)/shard_map/triangular_solve/custom-call.3 | solution.py:88
  298.6 9.8 %custom-call.43 = f32[1,128,128]{1,2,0:T(8,128)S(1)} custom-call(f32[1,128,128]{2,1,0:T(8,128)S(1)} %get-tuple-element.20), custom_call_target="InvertDiagBlocksLowerTriangular" | custom-call | tf_op jit(solution)/shard_map/triangular_solve/custom-call.2 | solution.py:84
  308.9 2.6 fusion.35
  311.7 1.9 fusion.189
  316.2 41.4 %psum.31 = f32[128,80]{0,1:T(8,128)S(1)} all-reduce(f32[128,80]{0,1:T(8,128)S(1)} %broadcast_select_fusion), channel_id=1, replica_groups=mesh['mem'=4,'sub'=8] {'mem','sub'}, use_global_device_ids=true, to_apply=%region_11.17 | all-reduce | flops 10240 | bytes 81920 | tf_op jit(solution)/shard_map/psum | solution.py:169
  358.1 11.7 %cholesky.107 = f32[128,128]{1,0:T(8,128)S(1)} custom-call(f32[128,128]{1,0:T(8,128)S(1)} %copy.54), custom_call_target="Cholesky" | custom-call | tf_op jit(solution)/shard_map/jit(cholesky)/cholesky | solution.py:81
  371.3 9.8 %custom-call.48 = f32[1,128,128]{1,2,0:T(8,128)S(1)} custom-call(f32[1,128,128]{2,1,0:T(8,128)S(1)} %get-tuple-element.19), custom_call_target="InvertDiagBlocksLowerTriangular" | custom-call | tf_op jit(solution)/shard_map/triangular_solve/custom-call.3 | solution.py:88
  381.3 9.8 %custom-call.47 = f32[1,128,128]{1,2,0:T(8,128)S(1)} custom-call(f32[1,128,128]{2,1,0:T(8,128)S(1)} %get-tuple-element.18), custom_call_target="InvertDiagBlocksLowerTriangular" | custom-call | tf_op jit(solution)/shard_map/triangular_solve/custom-call.2 | solution.py:84
  391.6 2.6 fusion.33
  394.5 1.7 fusion.20
  (158 shorter events, 34.5 us)
Async XLA Ops:
  0.0 15.6 %copy-start.8 = (f32[20,1,24,512]{3,2,1,0:T(8,128)S(1)}, f32[20,1,24,512]{3,2,1,0:T(8,128)}, u32[]{:S(2)}) copy-start(f32[20,1,24,512]{3,2,1,0:T(8,128)} %param.18) | copy-start | bytes 2949124
  0.0 47.4 %collective-permute-start = (f32[20,1,24,512]{3,2,1,0:T(8,128)}, f32[20,1,24,512]{3,2,1,0:T(8,128)}, u32[]{:S(2)}, u32[]{:S(2)}) collective-permute-start(f32[20,1,24,512]{3,2,1,0:T(8,128)} %param.18), channel_id=1, source_target_pairs={{0,1},{1,2},{2,3},{3,4},{4,5},{5,6},{6,7},{8,9},{9,10},{10,11},{11... | collective-permute-start | bytes 2949128 | tf_op jit(solution)/shard_map/ppermute | solution.py:28
  5.9 41.4 %collective-permute-start.1 = (f32[20,1,24,512]{3,2,1,0:T(8,128)}, f32[20,1,24,512]{3,2,1,0:T(8,128)}, u32[]{:S(2)}, u32[]{:S(2)}) collective-permute-start(f32[20,1,24,512]{3,2,1,0:T(8,128)} %param.18), channel_id=1, source_target_pairs={{1,0},{2,1},{3,2},{4,3},{5,4},{6,5},{7,6},{9,8},{10,9},{11,10},{12... | collective-permute-start | bytes 2949128 | tf_op jit(solution)/shard_map/ppermute | solution.py:29
  15.6 31.8 %copy-start.13 = (f32[1,512]{1,0:T(1,128)S(1)}, f32[1,512]{1,0:T(1,128)}, u32[]{:S(2)}) copy-start(f32[1,512]{1,0:T(1,128)} %param.21) | copy-start | bytes 6148
  51.1 8.2 %collective-permute-start.4 = (f32[20,1,24,128]{3,2,0,1:T(8,128)S(1)}, f32[20,1,24,128]{3,2,0,1:T(8,128)S(1)}, u32[]{:S(2)}, u32[]{:S(2)}) collective-permute-start(f32[20,1,24,128]{3,2,0,1:T(8,128)S(1)} %bitcast.355), channel_id=1, source_target_pairs={{0,24},{8,16},{16,8},{24,0},{1,25},{9,17},{17,9},{25,1},{2,26},{10... | collective-permute-start | bytes 737288 | tf_op jit(solution)/shard_map/ppermute | solution.py:151
  51.2 13.4 %collective-permute-start.3 = (f32[20,1,24,128]{3,2,0,1:T(8,128)S(1)}, f32[20,1,24,128]{3,2,0,1:T(8,128)S(1)}, u32[]{:S(2)}, u32[]{:S(2)}) collective-permute-start(f32[20,1,24,128]{3,2,0,1:T(8,128)S(1)} %bitcast.353), channel_id=1, source_target_pairs={{0,16},{8,24},{16,0},{24,8},{1,17},{9,25},{17,1},{25,9},{2,18},{10... | collective-permute-start | bytes 737288 | tf_op jit(solution)/shard_map/ppermute | solution.py:151
  52.7 11.9 %collective-permute-start.2 = (f32[20,1,24,128]{3,2,0,1:T(8,128)S(1)}, f32[20,1,24,128]{3,2,0,1:T(8,128)S(1)}, u32[]{:S(2)}, u32[]{:S(2)}) collective-permute-start(f32[20,1,24,128]{3,2,0,1:T(8,128)S(1)} %bitcast.352), channel_id=1, source_target_pairs={{0,8},{8,0},{16,24},{24,16},{1,9},{9,1},{17,25},{25,17},{2,10},{10... | collective-permute-start | bytes 737288 | tf_op jit(solution)/shard_map/ppermute | solution.py:151
  65.4 0.9 copy-start
  67.1 1.6 copy-start.17
  67.1 43.6 %copy-start.1 = (f32[4,20,24,128]{3,2,1,0:T(8,128)S(1)}, f32[4,20,24,128]{3,2,1,0:T(8,128)}, u32[]{:S(2)}) copy-start(f32[4,20,24,128]{3,2,1,0:T(8,128)} %copy-done) | copy-start | bytes 2949124
  67.2 43.8 %copy-start.25 = (f32[128]{0:T(128)S(1)}, f32[128]{0:T(128)}, u32[]{:S(2)}) copy-start(f32[128]{0:T(128)} %get-tuple-element.56) | copy-start | bytes 1540
  67.2 56.7 %copy-start.24 = (f32[128]{0:T(128)S(1)}, f32[128]{0:T(128)}, u32[]{:S(2)}) copy-start(f32[128]{0:T(128)} %get-tuple-element.53) | copy-start | bytes 1540
  68.6 75.8 %copy-start.11 = (f32[4,128]{1,0:T(4,128)S(1)}, f32[4,128]{1,0:T(4,128)}, u32[]{:S(2)}) copy-start(f32[4,128]{1,0:T(4,128)} %param.23) | copy-start | bytes 6148
  150.6 0.9 copy-start.4
  151.6 0.8 copy-start.9
  152.4 0.7 copy-start.16
  152.4 42.1 %copy-start.23 = (f32[128]{0:T(128)S(1)}, f32[128]{0:T(128)}, u32[]{:S(2)}) copy-start(f32[128]{0:T(128)} %get-tuple-element.55) | copy-start | bytes 1540
  152.4 55.0 %copy-start.22 = (f32[128]{0:T(128)S(1)}, f32[128]{0:T(128)}, u32[]{:S(2)}) copy-start(f32[128]{0:T(128)} %get-tuple-element.52) | copy-start | bytes 1540
  152.4 75.8 %copy-start.10 = (f32[24,128]{1,0:T(8,128)S(1)}, f32[24,128]{1,0:T(8,128)}, u32[]{:S(2)}) copy-start(f32[24,128]{1,0:T(8,128)} %get-tuple-element.68) | copy-start | bytes 36868
  152.4 75.8 %copy-start.5 = (f32[80,24,128]{2,0,1:T(8,128)S(1)}, f32[80,24,128]{2,0,1:T(8,128)}, u32[]{:S(2)}) copy-start(f32[80,24,128]{2,0,1:T(8,128)} %copy-done.4) | copy-start | bytes 2949124
  233.0 0.9 copy-start.6
  234.8 0.7 copy-start.15
  234.8 40.2 %copy-start.21 = (f32[128]{0:T(128)S(1)}, f32[128]{0:T(128)}, u32[]{:S(2)}) copy-start(f32[128]{0:T(128)} %get-tuple-element.57) | copy-start | bytes 1540
  234.8 53.1 %copy-start.20 = (f32[128]{0:T(128)S(1)}, f32[128]{0:T(128)}, u32[]{:S(2)}) copy-start(f32[128]{0:T(128)} %get-tuple-element.51) | copy-start | bytes 1540
  234.8 74.0 %copy-start.7 = (f32[80,24,128]{2,0,1:T(8,128)S(1)}, f32[80,24,128]{2,0,1:T(8,128)}, u32[]{:S(2)}) copy-start(f32[80,24,128]{2,0,1:T(8,128)} %copy-done.6) | copy-start | bytes 2949124
  313.7 0.9 copy-start.2
  315.5 0.7 copy-start.14
  315.5 42.1 %copy-start.19 = (f32[128]{0:T(128)S(1)}, f32[128]{0:T(128)}, u32[]{:S(2)}) copy-start(f32[128]{0:T(128)} %get-tuple-element.54) | copy-start | bytes 1540
  315.5 55.1 %copy-start.18 = (f32[128]{0:T(128)S(1)}, f32[128]{0:T(128)}, u32[]{:S(2)}) copy-start(f32[128]{0:T(128)} %get-tuple-element.50) | copy-start | bytes 1540
  315.5 75.7 %copy-start.12 = (f32[4,128]{1,0:T(4,128)S(1)}, f32[4,128]{1,0:T(4,128)}, u32[]{:S(2)}) copy-start(f32[4,128]{1,0:T(4,128)} %param.23) | copy-start | bytes 6148
  315.5 76.0 %copy-start.3 = (f32[80,24,128]{2,0,1:T(8,128)S(1)}, f32[80,24,128]{2,0,1:T(8,128)}, u32[]{:S(2)}) copy-start(f32[80,24,128]{2,0,1:T(8,128)} %copy-done.2) | copy-start | bytes 2949124
